TPU v7x, 32 devices: a whole 2x2x4 slice. The times are simulated.
32 devices in a mesh: gx: 4 (over z), gy: 4 (over y, x), gz: 2 (over core).
Axes of the slice: x: 2, y: 2, z: 4, core: 2. Of those that a mesh axis runs over, the one named last changes fastest.
Arguments:
- source_points: float32 [3, 13, 4, 16, 4, 512], P(None, None, 'gx', 'gy', 'gz'), may hold values from -3 to 3
- target_points: float32 [3, 13, 4, 16, 4, 512], P(None, None, 'gx', 'gy', 'gz'), may hold values from -3 to 3
- normals: float32 [3, 13, 4, 16, 4, 512], P(None, None, 'gx', 'gy', 'gz'), may hold values from -4 to 4
- weights: float32 [13, 4, 16, 4, 512], P(None, 'gx', 'gy', 'gz'), may hold values from 0.1 to 1
- blocks: int32 [13, 4, 16, 4], P(None, 'gx', 'gy', 'gz'), may hold values from 0 to 2
- affines: float32 [12, 4, 16, 4], P(None, 'gx', 'gy', 'gz'), may hold values from -0.5 to 0.5
- anchor: int32 [1], replicated, may hold values from 0 to 255
Outputs:
- update: float32 [12, 4, 16, 4], P(None, 'gx', 'gy', 'gz')
- residual: float32 [12, 4, 16, 4], P(None, 'gx', 'gy', 'gz')
Inputs may be any that keep to these rules, and one draw needn't show every extreme that they name: `blocks`: number of 256-point correspondence blocks of the correlation; entries of correlations whose second tile lies outside the grid are not read. `anchor`: a tile index (x 16 + y) * 4 + z.
All inputs are finite; a program needn't handle non-finite values.
Results may differ from a plain program's by a relative error of at most 0.0003.
Values sent between devices are 32-bit elements; how exact they have to be, the bound alone decides.
A program may use at most 128 MiB of HBM per device.

v0:
```python
import jax
import jax.numpy as jnp
from jax import lax
from jax.sharding import PartitionSpec as P

BLOCK = 256
ITERS = 10
SPACING = 0.5
DAMPING = 1.0
OFFSETS = (
    (1, 0, 0),
    (0, 1, 0),
    (0, 0, 1),
    (1, 1, -1),
    (1, -1, 1),
    (-1, 1, 1),
    (1, 1, 0),
    (1, 0, 1),
    (0, 1, 1),
    (1, 1, 1),
    (1, -1, 0),
    (0, 1, -1),
    (-1, 0, 1),
)


def padded(value, sides, width):
    for axis, dim in sides:
        devices, length = (lax.axis_size(axis), value.shape[dim])
        up = [(i, (i + 1) % devices) for i in range(devices - 1)]
        down = [(j, i) for i, j in up]
        last = lax.slice_in_dim(value, length - width, length, axis=dim)
        first = lax.slice_in_dim(value, 0, width, axis=dim)
        before = lax.ppermute(last, axis, up)
        after = lax.ppermute(first, axis, down)
        value = jnp.concatenate([before, value, after], axis=dim)
    return value


def spot(offset, rank, first, lengths):
    picks = [slice(None)] * rank
    for axis in range(3):
        picks[first + axis] = slice(1 + offset[axis], 1 + offset[axis] + lengths[axis])
    return tuple(picks)


def window(values, offset, first):
    lengths = tuple((values.shape[first + axis] - 2 for axis in range(3)))
    return values[spot(offset, values.ndim, first, lengths)]


def lifted(points):
    return jnp.concatenate([points, jnp.ones((1,) + points.shape[1:], points.dtype)], axis=0)


def mapped(affine, lifted_points):
    matrix = affine.reshape((3, 4) + affine.shape[1:]) + jnp.eye(3, 4, dtype=affine.dtype).reshape(
        3, 4, 1, 1, 1
    )
    return jnp.einsum("cexyz,exyzp->cxyzp", matrix, lifted_points, precision=lax.Precision.HIGHEST)


def correlation_terms(source, target, normal, weight, affine_here, affine_there, offset):
    exact = lax.Precision.HIGHEST
    source_lift = lifted(source)
    target_lift = lifted(target)
    stride = jnp.asarray(offset, source.dtype).reshape(3, 1, 1, 1, 1) * SPACING
    misfit = jnp.sum(
        normal * (mapped(affine_here, source_lift) - mapped(affine_there, target_lift) - stride),
        axis=0,
    )
    layout = (12,) + source.shape[1:]
    rows_here = (normal[:, None] * source_lift[None]).reshape(layout)
    rows_there = -(normal[:, None] * target_lift[None]).reshape(layout)
    weighted_here = rows_here * weight
    weighted_there = rows_there * weight
    block_here = jnp.einsum("axyzp,bxyzp->abxyz", weighted_here, rows_here, precision=exact)
    block_pair = jnp.einsum("axyzp,bxyzp->abxyz", weighted_here, rows_there, precision=exact)
    block_there = jnp.einsum("axyzp,bxyzp->abxyz", weighted_there, rows_there, precision=exact)
    pull_here = jnp.einsum("axyzp,xyzp->axyz", weighted_here, misfit, precision=exact)
    pull_there = jnp.einsum("axyzp,xyzp->axyz", weighted_there, misfit, precision=exact)
    return (block_here, block_pair, block_there, pull_here, pull_there)


def invert_blocks(blocks):
    left = blocks
    right = jnp.broadcast_to(
        jnp.eye(12, dtype=blocks.dtype).reshape((12, 12) + (1,) * (blocks.ndim - 2)), blocks.shape
    )
    for pivot in range(12):
        factor = 1.0 / left[pivot, pivot]
        row_left = left[pivot] * factor
        row_right = right[pivot] * factor
        column = left[:, pivot]
        left = left - column[:, None] * row_left[None]
        right = right - column[:, None] * row_right[None]
        left = left.at[pivot].set(row_left)
        right = right.at[pivot].set(row_right)
    return right


def fold_back(extended):
    rims = jnp.concatenate([extended[:, :1], extended[:, -1:]], axis=1)
    came = padded(rims, (("gx", 1),), 1)
    inner = extended[:, 1:-1]
    inner = inner.at[:, :1].add(came[:, :1]).at[:, -1:].add(came[:, -1:])
    rims = jnp.concatenate([inner[:, :, :1], inner[:, :, -1:]], axis=2)
    came = padded(rims, (("gy", 2),), 1)
    inner = inner[:, :, 1:-1]
    inner = inner.at[:, :, :1].add(came[:, :, :1]).at[:, :, -1:].add(came[:, :, -1:])
    rims = jnp.concatenate([inner[:, :, :, :1], inner[:, :, :, -1:]], axis=3)
    came = padded(rims, (("gz", 3),), 1)
    inner = inner[:, :, :, 1:-1]
    return inner.at[:, :, :, :1].add(came[:, :, :, :1]).at[:, :, :, -1:].add(came[:, :, :, -1:])


def beside_all(vector):
    return padded(vector, (("gx", 1), ("gy", 2), ("gz", 3)), 1)


def both_products(residual, scaled, image):
    return lax.psum((jnp.sum(residual * scaled), jnp.sum(image * scaled)), ("gx", "gy", "gz"))


def on_device(source_points, target_points, normals, weights, blocks, affines, anchor):
    exact = lax.Precision.HIGHEST
    directions = source_points.shape[1]
    tile_x, tile_y, tile_z = (
        source_points.shape[2],
        source_points.shape[3],
        source_points.shape[4],
    )
    points = source_points.shape[5]
    lengths = (tile_x, tile_y, tile_z)
    span_x = tile_x * lax.axis_size("gx")
    span_y = tile_y * lax.axis_size("gy")
    span_z = tile_z * lax.axis_size("gz")
    wide_x = lax.axis_index("gx") * tile_x - 1 + jnp.arange(tile_x + 2, dtype=jnp.int32)
    wide_y = lax.axis_index("gy") * tile_y - 1 + jnp.arange(tile_y + 2, dtype=jnp.int32)
    wide_z = lax.axis_index("gz") * tile_z - 1 + jnp.arange(tile_z + 2, dtype=jnp.int32)
    inside_x = ((wide_x >= 0) & (wide_x < span_x)).astype(jnp.float32).reshape(-1, 1, 1)
    inside_y = ((wide_y >= 0) & (wide_y < span_y)).astype(jnp.float32).reshape(1, -1, 1)
    inside_z = ((wide_z >= 0) & (wide_z < span_z)).astype(jnp.float32).reshape(1, 1, -1)
    inside_wide = inside_x * inside_y * inside_z
    flat_wide = (
        wide_x.reshape(-1, 1, 1) * span_y + wide_y.reshape(1, -1, 1)
    ) * span_z + wide_z.reshape(1, 1, -1)
    keep_wide = inside_wide * (flat_wide != anchor[0]).astype(jnp.float32)
    keep = keep_wide[1:-1, 1:-1, 1:-1]
    gathered = (
        padded(
            target_points.reshape((3 * directions, tile_x, tile_y, tile_z, points)),
            (("gx", 1), ("gy", 2), ("gz", 3)),
            1,
        ),
        padded(
            affines.reshape((12, tile_x, tile_y, tile_z, 1)), (("gx", 1), ("gy", 2), ("gz", 3)), 1
        ),
    )
    target_wide = gathered[0].reshape((3, directions) + gathered[0].shape[1:])
    affine_wide = gathered[1][..., 0]
    slots = jnp.arange(points, dtype=jnp.int32).reshape(1, 1, 1, points)
    extended = (tile_x + 2, tile_y + 2, tile_z + 2)
    diag = jnp.zeros((12, 12) + lengths, jnp.float32)
    pull = jnp.zeros((12,) + lengths, jnp.float32)
    back_blocks = jnp.zeros((156,) + extended, jnp.float32)
    pairs = []
    for index, offset in enumerate(OFFSETS):
        inside = window(inside_wide, offset, 0)
        live = (slots < BLOCK * blocks[index][..., None]).astype(jnp.float32) * inside[..., None]
        target = window(target_wide[:, index], offset, 1)
        block_here, block_pair, block_there, pull_here, pull_there = correlation_terms(
            source_points[:, index],
            target,
            normals[:, index],
            weights[index] * live,
            affines,
            window(affine_wide, offset, 1),
            offset,
        )
        block_pair = block_pair * (keep * window(keep_wide, offset, 0))
        diag = diag + block_here
        pull = pull + pull_here
        pairs.append(block_pair)
        place = spot(offset, 4, 1, lengths)
        back_blocks = back_blocks.at[place].add(
            jnp.concatenate([block_there.reshape((144,) + lengths), pull_there], axis=0)
        )
    coupling = jnp.stack(pairs)
    folded = fold_back(back_blocks)
    diag = diag + folded[:144].reshape((12, 12) + lengths)
    pull = pull + folded[144:156]
    identity = jnp.eye(12, dtype=jnp.float32).reshape(12, 12, 1, 1, 1)
    diag = keep * (diag + DAMPING * identity) + (1.0 - keep) * identity
    rhs = -(keep * pull)
    inverse = invert_blocks(diag)

    def operate(vector):
        wide = beside_all(vector)
        ahead = jnp.stack([window(wide, offset, 1) for offset in OFFSETS])
        result = jnp.einsum("abxyz,bxyz->axyz", diag, vector, precision=exact)
        result = result + jnp.einsum("dabxyz,dbxyz->axyz", coupling, ahead, precision=exact)
        sent = jnp.einsum("dbaxyz,bxyz->daxyz", coupling, vector, precision=exact)
        back = jnp.zeros((12,) + extended, jnp.float32)
        for index, offset in enumerate(OFFSETS):
            back = back.at[spot(offset, 4, 1, lengths)].add(sent[index])
        return result + fold_back(back)

    def precondition(vector):
        return jnp.einsum("abxyz,bxyz->axyz", inverse, vector, precision=exact)

    update = jnp.zeros_like(rhs)
    residual = rhs
    scaled = precondition(residual)
    image = operate(scaled)
    inner, product = both_products(residual, scaled, image)
    alpha = inner / product
    direction, along = (scaled, image)
    for step in range(ITERS):
        update = update + alpha * direction
        residual = residual - alpha * along
        if step + 1 < ITERS:
            scaled = precondition(residual)
            image = operate(scaled)
            inner_next, product = both_products(residual, scaled, image)
            ratio = inner_next / inner
            alpha = inner_next / (product - ratio * inner_next / alpha)
            direction = scaled + ratio * direction
            along = image + ratio * along
            inner = inner_next
    return (update, residual)


def solution(mesh):
    placed = (
        P(None, None, "gx", "gy", "gz", None),
        P(None, None, "gx", "gy", "gz", None),
        P(None, None, "gx", "gy", "gz", None),
        P(None, "gx", "gy", "gz", None),
        P(None, "gx", "gy", "gz"),
        P(None, "gx", "gy", "gz"),
        P(),
    )
    return jax.shard_map(
        on_device,
        mesh=mesh,
        in_specs=placed,
        out_specs=(P(None, "gx", "gy", "gz"), P(None, "gx", "gy", "gz")),
        check_vma=False,
    )
```

profile of v0, /device:TPU:0, one launch (start us, length us, event | category | flops | bytes accessed | tf_op | source)
XLA Modules:
  0.0 1302.6 jit_solution(10599703377848781927)
XLA Ops:
  162.1 5.6 pad_maximum_fusion
  199.2 11.4 fusion.203
  360.4 5.7 fusion.452
  393.3 5.3 collective-permute-done.27
  404.8 41.6 %all-reduce.46 = (f32[]{:T(128)}, f32[]{:T(128)}) all-reduce(f32[]{:T(128)} %get-tuple-element.2981, f32[]{:T(128)} %get-tuple-element.2980), channel_id=1, replica_groups=mesh['gx'=4,'gy'=4,'gz'=2] {'gx','gy','gz'}, use_global_device_ids=true, to_apply=%region_14.0 | all-reduce | flops 2 | bytes 16 | tf_op jit(solution)/shard_map/psum | solution.py:122
  454.0 5.7 fusion.446
  485.4 5.3 collective-permute-done.39
  497.0 41.6 %all-reduce.45 = (f32[]{:T(128)}, f32[]{:T(128)}) all-reduce(f32[]{:T(128)} %get-tuple-element.2979, f32[]{:T(128)} %get-tuple-element.2978), channel_id=1, replica_groups=mesh['gx'=4,'gy'=4,'gz'=2] {'gx','gy','gz'}, use_global_device_ids=true, to_apply=%region_18.0 | all-reduce | flops 2 | bytes 16 | tf_op jit(solution)/shard_map/psum | solution.py:122
  549.5 5.7 fusion.440
  580.9 5.3 collective-permute-done.51
  592.4 41.6 %all-reduce.44 = (f32[]{:T(128)}, f32[]{:T(128)}) all-reduce(f32[]{:T(128)} %get-tuple-element.2977, f32[]{:T(128)} %get-tuple-element.2976), channel_id=1, replica_groups=mesh['gx'=4,'gy'=4,'gz'=2] {'gx','gy','gz'}, use_global_device_ids=true, to_apply=%region_22.0 | all-reduce | flops 2 | bytes 16 | tf_op jit(solution)/shard_map/psum | solution.py:122
  644.2 5.7 fusion.434
  675.6 5.3 collective-permute-done.63
  687.6 41.6 %all-reduce.43 = (f32[]{:T(128)}, f32[]{:T(128)}) all-reduce(f32[]{:T(128)} %get-tuple-element.2975, f32[]{:T(128)} %get-tuple-element.2974), channel_id=1, replica_groups=mesh['gx'=4,'gy'=4,'gz'=2] {'gx','gy','gz'}, use_global_device_ids=true, to_apply=%region_26.0 | all-reduce | flops 2 | bytes 16 | tf_op jit(solution)/shard_map/psum | solution.py:122
  739.2 5.7 fusion.428
  770.6 5.3 collective-permute-done.75
  782.1 41.6 %all-reduce.42 = (f32[]{:T(128)}, f32[]{:T(128)}) all-reduce(f32[]{:T(128)} %get-tuple-element.2973, f32[]{:T(128)} %get-tuple-element.2972), channel_id=1, replica_groups=mesh['gx'=4,'gy'=4,'gz'=2] {'gx','gy','gz'}, use_global_device_ids=true, to_apply=%region_30.0 | all-reduce | flops 2 | bytes 16 | tf_op jit(solution)/shard_map/psum | solution.py:122
  833.8 5.7 fusion.422
  865.2 5.3 collective-permute-done.87
  877.0 41.6 %all-reduce.41 = (f32[]{:T(128)}, f32[]{:T(128)}) all-reduce(f32[]{:T(128)} %get-tuple-element.2971, f32[]{:T(128)} %get-tuple-element.2970), channel_id=1, replica_groups=mesh['gx'=4,'gy'=4,'gz'=2] {'gx','gy','gz'}, use_global_device_ids=true, to_apply=%region_34.0 | all-reduce | flops 2 | bytes 16 | tf_op jit(solution)/shard_map/psum | solution.py:122
  928.6 5.7 fusion.416
  960.0 5.3 collective-permute-done.99
  971.5 41.6 %all-reduce.40 = (f32[]{:T(128)}, f32[]{:T(128)}) all-reduce(f32[]{:T(128)} %get-tuple-element.2969, f32[]{:T(128)} %get-tuple-element.2968), channel_id=1, replica_groups=mesh['gx'=4,'gy'=4,'gz'=2] {'gx','gy','gz'}, use_global_device_ids=true, to_apply=%region_38.0 | all-reduce | flops 2 | bytes 16 | tf_op jit(solution)/shard_map/psum | solution.py:122
  1023.2 5.7 fusion.410
  1054.6 5.3 collective-permute-done.111
  1066.4 41.6 %all-reduce.39 = (f32[]{:T(128)}, f32[]{:T(128)}) all-reduce(f32[]{:T(128)} %get-tuple-element.2967, f32[]{:T(128)} %get-tuple-element.2966), channel_id=1, replica_groups=mesh['gx'=4,'gy'=4,'gz'=2] {'gx','gy','gz'}, use_global_device_ids=true, to_apply=%region_42.0 | all-reduce | flops 2 | bytes 16 | tf_op jit(solution)/shard_map/psum | solution.py:122
  1118.1 5.7 fusion.404
  1149.5 5.3 collective-permute-done.123
  1161.0 41.6 %all-reduce.38 = (f32[]{:T(128)}, f32[]{:T(128)}) all-reduce(f32[]{:T(128)} %get-tuple-element.2965, f32[]{:T(128)} %get-tuple-element.2964), channel_id=1, replica_groups=mesh['gx'=4,'gy'=4,'gz'=2] {'gx','gy','gz'}, use_global_device_ids=true, to_apply=%region_46.0 | all-reduce | flops 2 | bytes 16 | tf_op jit(solution)/shard_map/psum | solution.py:122
  1212.7 5.7 fusion.398
  1244.1 5.3 collective-permute-done.135
  1255.7 41.6 %all-reduce.37 = (f32[]{:T(128)}, f32[]{:T(128)}) all-reduce(f32[]{:T(128)} %get-tuple-element.2963, f32[]{:T(128)} %get-tuple-element.2962), channel_id=1, replica_groups=mesh['gx'=4,'gy'=4,'gz'=2] {'gx','gy','gz'}, use_global_device_ids=true, to_apply=%region_50.0 | all-reduce | flops 2 | bytes 16 | tf_op jit(solution)/shard_map/psum | solution.py:122
  (1706 shorter events, 713.1 us)
Async XLA Ops:
  0.6 51.8 %collective-permute-start = (f32[39,1,4,2,512]{4,3,2,1,0:T(2,128)}, f32[39,1,4,2,512]{4,3,2,1,0:T(2,128)S(1)}, u32[]{:S(2)}, u32[]{:S(2)}) collective-permute-start(f32[39,1,4,2,512]{4,3,2,1,0:T(2,128)} %bitcast.2152), channel_id=1, source_target_pairs={{0,8},{8,16},{16,24},{1,9},{9,17},{17,25},{2,10},{10,18},{18,26},{... | collective-permute-start | bytes 1916936 | tf_op jit(solution)/shard_map/ppermute | solution.py:34
  5.8 46.6 %collective-permute-start.1 = (f32[39,1,4,2,512]{4,3,2,1,0:T(2,128)}, f32[39,1,4,2,512]{4,3,2,1,0:T(2,128)S(1)}, u32[]{:S(2)}, u32[]{:S(2)}) collective-permute-start(f32[39,1,4,2,512]{4,3,2,1,0:T(2,128)} %bitcast.2153), channel_id=1, source_target_pairs={{8,0},{16,8},{24,16},{9,1},{17,9},{25,17},{10,2},{18,10},{26,18},{... | collective-permute-start | bytes 1916936 | tf_op jit(solution)/shard_map/ppermute | solution.py:35
  7.8 123.7 %collective-permute-start.6 = (f32[12,1,4,2,1]{0,2,4,3,1:T(4,128)S(1)}, f32[12,1,4,2,1]{0,2,4,3,1:T(4,128)}, u32[]{:S(2)}, u32[]{:S(2)}) collective-permute-start(f32[12,1,4,2,1]{0,2,4,3,1:T(4,128)S(1)} %bitcast.2434), channel_id=1, source_target_pairs={{0,8},{8,16},{16,24},{1,9},{9,17},{17,25},{2,10},{10,18},{18,26},{... | collective-permute-start | bytes 1160 | tf_op jit(solution)/shard_map/ppermute | solution.py:34
  12.9 118.5 %collective-permute-start.7 = (f32[12,1,4,2,1]{0,2,4,3,1:T(4,128)S(1)}, f32[12,1,4,2,1]{0,2,4,3,1:T(4,128)}, u32[]{:S(2)}, u32[]{:S(2)}) collective-permute-start(f32[12,1,4,2,1]{0,2,4,3,1:T(4,128)S(1)} %bitcast.2435), channel_id=1, source_target_pairs={{8,0},{16,8},{24,16},{9,1},{17,9},{25,17},{10,2},{18,10},{26,18},{... | collective-permute-start | bytes 1160 | tf_op jit(solution)/shard_map/ppermute | solution.py:35
  53.8 64.2 %collective-permute-start.2 = (f32[39,3,1,2,512]{4,3,2,1,0:T(2,128)}, f32[39,3,1,2,512]{4,3,2,1,0:T(2,128)S(1)}, u32[]{:S(2)}, u32[]{:S(2)}) collective-permute-start(f32[39,3,1,2,512]{4,3,2,1,0:T(2,128)} %get-tuple-element.3030), channel_id=1, source_target_pairs={{0,2},{2,4},{4,6},{1,3},{3,5},{5,7},{8,10},{10,12},{12,14},{9,11},... | collective-permute-start | bytes 1437704 | tf_op jit(solution)/shard_map/ppermute | solution.py:34
  57.2 60.7 %collective-permute-start.3 = (f32[39,3,1,2,512]{4,3,2,1,0:T(2,128)}, f32[39,3,1,2,512]{4,3,2,1,0:T(2,128)S(1)}, u32[]{:S(2)}, u32[]{:S(2)}) collective-permute-start(f32[39,3,1,2,512]{4,3,2,1,0:T(2,128)} %get-tuple-element.3031), channel_id=1, source_target_pairs={{2,0},{4,2},{6,4},{3,1},{5,3},{7,5},{10,8},{12,10},{14,12},{11,9},... | collective-permute-start | bytes 1437704 | tf_op jit(solution)/shard_map/ppermute | solution.py:35
  123.4 38.7 %collective-permute-start.4 = (f32[39,3,6,1,512]{4,3,2,1,0:T(1,128)}, f32[39,3,6,1,512]{4,3,2,1,0:T(1,128)}, u32[]{:S(2)}, u32[]{:S(2)}) collective-permute-start(f32[39,3,6,1,512]{4,3,2,1,0:T(1,128)} %get-tuple-element.3028), channel_id=1, source_target_pairs={{0,1},{2,3},{4,5},{6,7},{8,9},{10,11},{12,13},{14,15},{16,17},{18,... | collective-permute-start | bytes 4313096 | tf_op jit(solution)/shard_map/ppermute | solution.py:34
  125.8 36.3 %collective-permute-start.5 = (f32[39,3,6,1,512]{4,3,2,1,0:T(1,128)}, f32[39,3,6,1,512]{4,3,2,1,0:T(1,128)}, u32[]{:S(2)}, u32[]{:S(2)}) collective-permute-start(f32[39,3,6,1,512]{4,3,2,1,0:T(1,128)} %get-tuple-element.3029), channel_id=1, source_target_pairs={{1,0},{3,2},{5,4},{7,6},{9,8},{11,10},{13,12},{15,14},{17,16},{19,... | collective-permute-start | bytes 4313096 | tf_op jit(solution)/shard_map/ppermute | solution.py:35
  276.6 50.9 %collective-permute-start.12 = (f32[156,1,6,4]{0,3,2,1:T(4,128)S(1)}, f32[156,1,6,4]{0,3,2,1:T(4,128)S(1)}, u32[]{:S(2)}, u32[]{:S(2)}) collective-permute-start(f32[156,1,6,4]{0,3,2,1:T(4,128)S(1)} %get-tuple-element.3070), channel_id=1, source_target_pairs={{0,8},{8,16},{16,24},{1,9},{9,17},{17,25},{2,10},{10,18},{18,26},{... | collective-permute-start | bytes 44936 | tf_op jit(solution)/shard_map/ppermute | solution.py:34
  281.1 46.4 %collective-permute-start.13 = (f32[156,1,6,4]{0,3,2,1:T(4,128)S(1)}, f32[156,1,6,4]{0,3,2,1:T(4,128)S(1)}, u32[]{:S(2)}, u32[]{:S(2)}) collective-permute-start(f32[156,1,6,4]{0,3,2,1:T(4,128)S(1)} %get-tuple-element.3071), channel_id=1, source_target_pairs={{8,0},{16,8},{24,16},{9,1},{17,9},{25,17},{10,2},{18,10},{26,18},{... | collective-permute-start | bytes 44936 | tf_op jit(solution)/shard_map/ppermute | solution.py:35
  353.7 22.3 %collective-permute-start.18 = (f32[12,1,4,2]{0,3,2,1:T(2,128)S(1)}, f32[12,1,4,2]{0,3,2,1:T(2,128)S(1)}, u32[]{:S(2)}, u32[]{:S(2)}) collective-permute-start(f32[12,1,4,2]{0,3,2,1:T(2,128)S(1)} %bitcast.2227), channel_id=1, source_target_pairs={{8,0},{16,8},{24,16},{9,1},{17,9},{25,17},{10,2},{18,10},{26,18},{... | collective-permute-start | bytes 1160 | tf_op jit(solution)/shard_map/ppermute | solution.py:35
  355.0 21.0 %collective-permute-start.19 = (f32[12,1,4,2]{0,3,2,1:T(2,128)S(1)}, f32[12,1,4,2]{0,3,2,1:T(2,128)S(1)}, u32[]{:S(2)}, u32[]{:S(2)}) collective-permute-start(f32[12,1,4,2]{0,3,2,1:T(2,128)S(1)} %bitcast.2228), channel_id=1, source_target_pairs={{0,8},{8,16},{16,24},{1,9},{9,17},{17,25},{2,10},{10,18},{18,26},{... | collective-permute-start | bytes 1160 | tf_op jit(solution)/shard_map/ppermute | solution.py:34
  383.2 19.8 %collective-permute-start.22 = (f32[12,3,6,1]{0,3,2,1:T(1,128)S(1)}, f32[12,3,6,1]{0,3,2,1:T(1,128)S(1)}, u32[]{:S(2)}, u32[]{:S(2)}) collective-permute-start(f32[12,3,6,1]{0,3,2,1:T(1,128)S(1)} %get-tuple-element.3374), channel_id=1, source_target_pairs={{1,0},{3,2},{5,4},{7,6},{9,8},{11,10},{13,12},{15,14},{17,16},{19,... | collective-permute-start | bytes 2600 | tf_op jit(solution)/shard_map/ppermute | solution.py:35
  448.0 19.4 %collective-permute-start.30 = (f32[12,1,4,2]{0,3,2,1:T(2,128)S(1)}, f32[12,1,4,2]{0,3,2,1:T(2,128)S(1)}, u32[]{:S(2)}, u32[]{:S(2)}) collective-permute-start(f32[12,1,4,2]{0,3,2,1:T(2,128)S(1)} %bitcast.2238), channel_id=1, source_target_pairs={{8,0},{16,8},{24,16},{9,1},{17,9},{25,17},{10,2},{18,10},{26,18},{... | collective-permute-start | bytes 1160 | tf_op jit(solution)/shard_map/ppermute | solution.py:35
  474.9 20.3 %collective-permute-start.34 = (f32[12,3,6,1]{0,3,2,1:T(1,128)S(1)}, f32[12,3,6,1]{0,3,2,1:T(1,128)S(1)}, u32[]{:S(2)}, u32[]{:S(2)}) collective-permute-start(f32[12,3,6,1]{0,3,2,1:T(1,128)S(1)} %get-tuple-element.3371), channel_id=1, source_target_pairs={{1,0},{3,2},{5,4},{7,6},{9,8},{11,10},{13,12},{15,14},{17,16},{19,... | collective-permute-start | bytes 2600 | tf_op jit(solution)/shard_map/ppermute | solution.py:35
  543.4 19.4 %collective-permute-start.42 = (f32[12,1,4,2]{0,3,2,1:T(2,128)S(1)}, f32[12,1,4,2]{0,3,2,1:T(2,128)S(1)}, u32[]{:S(2)}, u32[]{:S(2)}) collective-permute-start(f32[12,1,4,2]{0,3,2,1:T(2,128)S(1)} %bitcast.2249), channel_id=1, source_target_pairs={{8,0},{16,8},{24,16},{9,1},{17,9},{25,17},{10,2},{18,10},{26,18},{... | collective-permute-start | bytes 1160 | tf_op jit(solution)/shard_map/ppermute | solution.py:35
  570.3 20.3 %collective-permute-start.46 = (f32[12,3,6,1]{0,3,2,1:T(1,128)S(1)}, f32[12,3,6,1]{0,3,2,1:T(1,128)S(1)}, u32[]{:S(2)}, u32[]{:S(2)}) collective-permute-start(f32[12,3,6,1]{0,3,2,1:T(1,128)S(1)} %get-tuple-element.3368), channel_id=1, source_target_pairs={{1,0},{3,2},{5,4},{7,6},{9,8},{11,10},{13,12},{15,14},{17,16},{19,... | collective-permute-start | bytes 2600 | tf_op jit(solution)/shard_map/ppermute | solution.py:35
  638.1 19.4 %collective-permute-start.54 = (f32[12,1,4,2]{0,3,2,1:T(2,128)S(1)}, f32[12,1,4,2]{0,3,2,1:T(2,128)S(1)}, u32[]{:S(2)}, u32[]{:S(2)}) collective-permute-start(f32[12,1,4,2]{0,3,2,1:T(2,128)S(1)} %bitcast.2260), channel_id=1, source_target_pairs={{8,0},{16,8},{24,16},{9,1},{17,9},{25,17},{10,2},{18,10},{26,18},{... | collective-permute-start | bytes 1160 | tf_op jit(solution)/shard_map/ppermute | solution.py:35
  665.0 20.7 %collective-permute-start.58 = (f32[12,3,6,1]{0,3,2,1:T(1,128)S(1)}, f32[12,3,6,1]{0,3,2,1:T(1,128)S(1)}, u32[]{:S(2)}, u32[]{:S(2)}) collective-permute-start(f32[12,3,6,1]{0,3,2,1:T(1,128)S(1)} %get-tuple-element.3365), channel_id=1, source_target_pairs={{1,0},{3,2},{5,4},{7,6},{9,8},{11,10},{13,12},{15,14},{17,16},{19,... | collective-permute-start | bytes 2600 | tf_op jit(solution)/shard_map/ppermute | solution.py:35
  666.3 19.4 %collective-permute-start.59 = (f32[12,3,6,1]{0,3,2,1:T(1,128)S(1)}, f32[12,3,6,1]{0,3,2,1:T(1,128)S(1)}, u32[]{:S(2)}, u32[]{:S(2)}) collective-permute-start(f32[12,3,6,1]{0,3,2,1:T(1,128)S(1)} %get-tuple-element.3364), channel_id=1, source_target_pairs={{0,1},{2,3},{4,5},{6,7},{8,9},{10,11},{12,13},{14,15},{16,17},{18,... | collective-permute-start | bytes 2600 | tf_op jit(solution)/shard_map/ppermute | solution.py:34
  733.2 19.4 %collective-permute-start.66 = (f32[12,1,4,2]{0,3,2,1:T(2,128)S(1)}, f32[12,1,4,2]{0,3,2,1:T(2,128)S(1)}, u32[]{:S(2)}, u32[]{:S(2)}) collective-permute-start(f32[12,1,4,2]{0,3,2,1:T(2,128)S(1)} %bitcast.2271), channel_id=1, source_target_pairs={{8,0},{16,8},{24,16},{9,1},{17,9},{25,17},{10,2},{18,10},{26,18},{... | collective-permute-start | bytes 1160 | tf_op jit(solution)/shard_map/ppermute | solution.py:35
  760.1 20.3 %collective-permute-start.70 = (f32[12,3,6,1]{0,3,2,1:T(1,128)S(1)}, f32[12,3,6,1]{0,3,2,1:T(1,128)S(1)}, u32[]{:S(2)}, u32[]{:S(2)}) collective-permute-start(f32[12,3,6,1]{0,3,2,1:T(1,128)S(1)} %get-tuple-element.3362), channel_id=1, source_target_pairs={{1,0},{3,2},{5,4},{7,6},{9,8},{11,10},{13,12},{15,14},{17,16},{19,... | collective-permute-start | bytes 2600 | tf_op jit(solution)/shard_map/ppermute | solution.py:35
  827.8 19.4 %collective-permute-start.78 = (f32[12,1,4,2]{0,3,2,1:T(2,128)S(1)}, f32[12,1,4,2]{0,3,2,1:T(2,128)S(1)}, u32[]{:S(2)}, u32[]{:S(2)}) collective-permute-start(f32[12,1,4,2]{0,3,2,1:T(2,128)S(1)} %bitcast.2282), channel_id=1, source_target_pairs={{8,0},{16,8},{24,16},{9,1},{17,9},{25,17},{10,2},{18,10},{26,18},{... | collective-permute-start | bytes 1160 | tf_op jit(solution)/shard_map/ppermute | solution.py:35
  854.7 20.5 %collective-permute-start.82 = (f32[12,3,6,1]{0,3,2,1:T(1,128)S(1)}, f32[12,3,6,1]{0,3,2,1:T(1,128)S(1)}, u32[]{:S(2)}, u32[]{:S(2)}) collective-permute-start(f32[12,3,6,1]{0,3,2,1:T(1,128)S(1)} %get-tuple-element.3359), channel_id=1, source_target_pairs={{1,0},{3,2},{5,4},{7,6},{9,8},{11,10},{13,12},{15,14},{17,16},{19,... | collective-permute-start | bytes 2600 | tf_op jit(solution)/shard_map/ppermute | solution.py:35
  922.6 19.4 %collective-permute-start.90 = (f32[12,1,4,2]{0,3,2,1:T(2,128)S(1)}, f32[12,1,4,2]{0,3,2,1:T(2,128)S(1)}, u32[]{:S(2)}, u32[]{:S(2)}) collective-permute-start(f32[12,1,4,2]{0,3,2,1:T(2,128)S(1)} %bitcast.2293), channel_id=1, source_target_pairs={{8,0},{16,8},{24,16},{9,1},{17,9},{25,17},{10,2},{18,10},{26,18},{... | collective-permute-start | bytes 1160 | tf_op jit(solution)/shard_map/ppermute | solution.py:35
  949.5 20.3 %collective-permute-start.94 = (f32[12,3,6,1]{0,3,2,1:T(1,128)S(1)}, f32[12,3,6,1]{0,3,2,1:T(1,128)S(1)}, u32[]{:S(2)}, u32[]{:S(2)}) collective-permute-start(f32[12,3,6,1]{0,3,2,1:T(1,128)S(1)} %get-tuple-element.3356), channel_id=1, source_target_pairs={{1,0},{3,2},{5,4},{7,6},{9,8},{11,10},{13,12},{15,14},{17,16},{19,... | collective-permute-start | bytes 2600 | tf_op jit(solution)/shard_map/ppermute | solution.py:35
  1017.2 19.4 %collective-permute-start.102 = (f32[12,1,4,2]{0,3,2,1:T(2,128)S(1)}, f32[12,1,4,2]{0,3,2,1:T(2,128)S(1)}, u32[]{:S(2)}, u32[]{:S(2)}) collective-permute-start(f32[12,1,4,2]{0,3,2,1:T(2,128)S(1)} %bitcast.2304), channel_id=1, source_target_pairs={{8,0},{16,8},{24,16},{9,1},{17,9},{25,17},{10,2},{18,10},{26,18},{... | collective-permute-start | bytes 1160 | tf_op jit(solution)/shard_map/ppermute | solution.py:35
  1044.1 20.5 %collective-permute-start.106 = (f32[12,3,6,1]{0,3,2,1:T(1,128)S(1)}, f32[12,3,6,1]{0,3,2,1:T(1,128)S(1)}, u32[]{:S(2)}, u32[]{:S(2)}) collective-permute-start(f32[12,3,6,1]{0,3,2,1:T(1,128)S(1)} %get-tuple-element.3353), channel_id=1, source_target_pairs={{1,0},{3,2},{5,4},{7,6},{9,8},{11,10},{13,12},{15,14},{17,16},{19,... | collective-permute-start | bytes 2600 | tf_op jit(solution)/shard_map/ppermute | solution.py:35
  1112.0 19.4 %collective-permute-start.114 = (f32[12,1,4,2]{0,3,2,1:T(2,128)S(1)}, f32[12,1,4,2]{0,3,2,1:T(2,128)S(1)}, u32[]{:S(2)}, u32[]{:S(2)}) collective-permute-start(f32[12,1,4,2]{0,3,2,1:T(2,128)S(1)} %bitcast.2315), channel_id=1, source_target_pairs={{8,0},{16,8},{24,16},{9,1},{17,9},{25,17},{10,2},{18,10},{26,18},{... | collective-permute-start | bytes 1160 | tf_op jit(solution)/shard_map/ppermute | solution.py:35
  1138.9 20.3 %collective-permute-start.118 = (f32[12,3,6,1]{0,3,2,1:T(1,128)S(1)}, f32[12,3,6,1]{0,3,2,1:T(1,128)S(1)}, u32[]{:S(2)}, u32[]{:S(2)}) collective-permute-start(f32[12,3,6,1]{0,3,2,1:T(1,128)S(1)} %get-tuple-element.3350), channel_id=1, source_target_pairs={{1,0},{3,2},{5,4},{7,6},{9,8},{11,10},{13,12},{15,14},{17,16},{19,... | collective-permute-start | bytes 2600 | tf_op jit(solution)/shard_map/ppermute | solution.py:35
  1206.6 19.4 %collective-permute-start.126 = (f32[12,1,4,2]{0,3,2,1:T(2,128)S(1)}, f32[12,1,4,2]{0,3,2,1:T(2,128)S(1)}, u32[]{:S(2)}, u32[]{:S(2)}) collective-permute-start(f32[12,1,4,2]{0,3,2,1:T(2,128)S(1)} %bitcast.2326), channel_id=1, source_target_pairs={{8,0},{16,8},{24,16},{9,1},{17,9},{25,17},{10,2},{18,10},{26,18},{... | collective-permute-start | bytes 1160 | tf_op jit(solution)/shard_map/ppermute | solution.py:35
  1233.5 20.3 %collective-permute-start.130 = (f32[12,3,6,1]{0,3,2,1:T(1,128)S(1)}, f32[12,3,6,1]{0,3,2,1:T(1,128)S(1)}, u32[]{:S(2)}, u32[]{:S(2)}) collective-permute-start(f32[12,3,6,1]{0,3,2,1:T(1,128)S(1)} %get-tuple-element.3347), channel_id=1, source_target_pairs={{1,0},{3,2},{5,4},{7,6},{9,8},{11,10},{13,12},{15,14},{17,16},{19,... | collective-permute-start | bytes 2600 | tf_op jit(solution)/shard_map/ppermute | solution.py:35
  (293 other events, 2996.9 us)
where the time goes:
time: 1320 us; the launch traced here: 1300 us
  blocking collectives  416 us (32%)
  starting transfers between devices  329 us (25%)
  local copies, waits for them, and re-layouts  174 us (13%)
  matrix products  170 us (13%)
  waiting for transfers between devices  92.3 us (7%)
  other arithmetic  75 us (6%)
  between operations  46.2 us (4%)
    psum x10, blocking collectives, both_products(): lax.psum((jnp.sum(residual * scaled), jnp.sum(image * scaled)), ('gx', 'g...  416 us
    ppermute x69, starting transfers between devices, padded(): before = lax.ppermute(last, axis, up)  240 us
    ppermute x69, starting transfers between devices, padded(): after = lax.ppermute(first, axis, down)  89.3 us
    ppermute x69, waiting for transfers between devices, padded(): after = lax.ppermute(first, axis, down)  79.4 us
    dot_general x10, matrix products, operate(): sent = jnp.einsum('dbaxyz,bxyz->daxyz', coupling, vector, precision=exact)  56.8 us
    another operation x65, local copies, waits for them, and re-layouts  28.1 us
  transfers between devices with their start and end apart: 138, of which 33 were waited for; matrix products, arithmetic and copies ran while one was open for 22% of the time, Pallas kernels for 0%

commit v1 on v0

--- a/solution.py
+++ b/solution.py
@@ -119,7 +119,9 @@
 
 
 def both_products(residual, scaled, image):
-    return lax.psum((jnp.sum(residual * scaled), jnp.sum(image * scaled)), ("gx", "gy", "gz"))
+    return lax.psum(
+        lax.psum((jnp.sum(residual * scaled), jnp.sum(image * scaled)), ("gy", "gz")), "gx"
+    )
 
 
 def on_device(source_points, target_points, normals, weights, blocks, affines, anchor):

time: 1320 us -> 1140 us (0.86)
  blocking collectives: 416 us -> 247 us
    psum x10 -> x20, blocking collectives: 416 us -> 247 us  [the longest x10 130 us: both_products(): lax.psum((jnp.sum(residual * scaled), jnp.sum(image * scaled)), ('gy', 'g...]
  transfers between devices with their start and end apart: 138 -> 138, of which waited for: 33 -> 33; matrix products, arithmetic and copies ran while one was open for 22% -> 25% of each run, Pallas kernels for 0% -> 0%
where the time goes in v1:
time: 1140 us; the launch traced here: 1120 us
  starting transfers between devices  329 us (29%)
  blocking collectives  247 us (22%)
  local copies, waits for them, and re-layouts  173 us (15%)
  matrix products  160 us (14%)
  waiting for transfers between devices  92.3 us (8%)
  other arithmetic  74.3 us (7%)
  between operations  47.6 us (4%)
    ppermute x69, starting transfers between devices, padded(): before = lax.ppermute(last, axis, up)  239 us
    psum x10, blocking collectives, both_products(): lax.psum((jnp.sum(residual * scaled), jnp.sum(image * scaled)), ('gy', 'g...  130 us
    psum x10, blocking collectives, both_products(): lax.psum(lax.psum((jnp.sum(residual * scaled), jnp.sum(image * scaled)),...  117 us
    ppermute x69, starting transfers between devices, padded(): after = lax.ppermute(first, axis, down)  89.3 us
    ppermute x69, waiting for transfers between devices, padded(): after = lax.ppermute(first, axis, down)  79.3 us
    dot_general x10, matrix products, operate(): sent = jnp.einsum('dbaxyz,bxyz->daxyz', coupling, vector, precision=exact)  56.8 us
    another operation x65, local copies, waits for them, and re-layouts  28.1 us
    dot_general x26, matrix products, mapped(): jnp.einsum('cexyz,exyzp->cxyzp', matrix, lifted_points, precision=lax.Pre...  24.5 us
  transfers between devices with their start and end apart: 138, of which 33 were waited for; matrix products, arithmetic and copies ran while one was open for 25% of the time, Pallas kernels for 0%

profile of v1, /device:TPU:0, one launch (start us, length us, event | category | flops | bytes accessed | tf_op | source)
XLA Modules:
  0.0 1122.0 jit_solution(4736576652661493938)
XLA Ops:
  162.4 5.5 pad_maximum_fusion
  350.7 5.7 fusion.452
  394.9 12.6 %all-reduce.46 = (f32[]{:T(128)}, f32[]{:T(128)}) all-reduce(f32[]{:T(128)} %get-tuple-element.2981, f32[]{:T(128)} %get-tuple-element.2980), channel_id=1, replica_groups=mesh['gx'=4,'gy'=4,'gz'=2] {'gy','gz'}, use_global_device_ids=true, to_apply=%region_14.0 | all-reduce | flops 2 | bytes 16 | tf_op jit(solution)/shard_map/psum | solution.py:123
  407.5 11.6 %all-reduce.56 = (f32[]{:T(128)}, f32[]{:T(128)}) all-reduce(f32[]{:T(128)} %get-tuple-element.3000, f32[]{:T(128)} %get-tuple-element.3001), channel_id=1, replica_groups=mesh['gx'=4,'gy'=4,'gz'=2] {'gx'}, use_global_device_ids=true, to_apply=%region_15.0 | all-reduce | flops 2 | bytes 16 | tf_op jit(solution)/shard_map/psum | solution.py:122
  426.8 5.7 fusion.446
  451.7 5.3 collective-permute-start.38
  470.2 13.1 %all-reduce.45 = (f32[]{:T(128)}, f32[]{:T(128)}) all-reduce(f32[]{:T(128)} %get-tuple-element.2979, f32[]{:T(128)} %get-tuple-element.2978), channel_id=1, replica_groups=mesh['gx'=4,'gy'=4,'gz'=2] {'gy','gz'}, use_global_device_ids=true, to_apply=%region_20.0 | all-reduce | flops 2 | bytes 16 | tf_op jit(solution)/shard_map/psum | solution.py:123
  483.3 11.7 %all-reduce.55 = (f32[]{:T(128)}, f32[]{:T(128)}) all-reduce(f32[]{:T(128)} %get-tuple-element.2998, f32[]{:T(128)} %get-tuple-element.2999), channel_id=1, replica_groups=mesh['gx'=4,'gy'=4,'gz'=2] {'gx'}, use_global_device_ids=true, to_apply=%region_21.0 | all-reduce | flops 2 | bytes 16 | tf_op jit(solution)/shard_map/psum | solution.py:122
  505.9 5.7 fusion.440
  548.4 13.0 %all-reduce.44 = (f32[]{:T(128)}, f32[]{:T(128)}) all-reduce(f32[]{:T(128)} %get-tuple-element.2977, f32[]{:T(128)} %get-tuple-element.2976), channel_id=1, replica_groups=mesh['gx'=4,'gy'=4,'gz'=2] {'gy','gz'}, use_global_device_ids=true, to_apply=%region_26.0 | all-reduce | flops 2 | bytes 16 | tf_op jit(solution)/shard_map/psum | solution.py:123
  561.5 11.6 %all-reduce.54 = (f32[]{:T(128)}, f32[]{:T(128)}) all-reduce(f32[]{:T(128)} %get-tuple-element.2996, f32[]{:T(128)} %get-tuple-element.2997), channel_id=1, replica_groups=mesh['gx'=4,'gy'=4,'gz'=2] {'gx'}, use_global_device_ids=true, to_apply=%region_27.0 | all-reduce | flops 2 | bytes 16 | tf_op jit(solution)/shard_map/psum | solution.py:122
  583.4 5.7 fusion.434
  626.0 13.1 %all-reduce.43 = (f32[]{:T(128)}, f32[]{:T(128)}) all-reduce(f32[]{:T(128)} %get-tuple-element.2975, f32[]{:T(128)} %get-tuple-element.2974), channel_id=1, replica_groups=mesh['gx'=4,'gy'=4,'gz'=2] {'gy','gz'}, use_global_device_ids=true, to_apply=%region_32.0 | all-reduce | flops 2 | bytes 16 | tf_op jit(solution)/shard_map/psum | solution.py:123
  639.1 11.7 %all-reduce.53 = (f32[]{:T(128)}, f32[]{:T(128)}) all-reduce(f32[]{:T(128)} %get-tuple-element.2994, f32[]{:T(128)} %get-tuple-element.2995), channel_id=1, replica_groups=mesh['gx'=4,'gy'=4,'gz'=2] {'gx'}, use_global_device_ids=true, to_apply=%region_33.0 | all-reduce | flops 2 | bytes 16 | tf_op jit(solution)/shard_map/psum | solution.py:122
  661.2 5.7 fusion.428
  703.8 13.0 %all-reduce.42 = (f32[]{:T(128)}, f32[]{:T(128)}) all-reduce(f32[]{:T(128)} %get-tuple-element.2973, f32[]{:T(128)} %get-tuple-element.2972), channel_id=1, replica_groups=mesh['gx'=4,'gy'=4,'gz'=2] {'gy','gz'}, use_global_device_ids=true, to_apply=%region_38.0 | all-reduce | flops 2 | bytes 16 | tf_op jit(solution)/shard_map/psum | solution.py:123
  716.8 11.6 %all-reduce.52 = (f32[]{:T(128)}, f32[]{:T(128)}) all-reduce(f32[]{:T(128)} %get-tuple-element.2992, f32[]{:T(128)} %get-tuple-element.2993), channel_id=1, replica_groups=mesh['gx'=4,'gy'=4,'gz'=2] {'gx'}, use_global_device_ids=true, to_apply=%region_39.0 | all-reduce | flops 2 | bytes 16 | tf_op jit(solution)/shard_map/psum | solution.py:122
  738.7 5.7 fusion.422
  781.3 13.1 %all-reduce.41 = (f32[]{:T(128)}, f32[]{:T(128)}) all-reduce(f32[]{:T(128)} %get-tuple-element.2971, f32[]{:T(128)} %get-tuple-element.2970), channel_id=1, replica_groups=mesh['gx'=4,'gy'=4,'gz'=2] {'gy','gz'}, use_global_device_ids=true, to_apply=%region_44.0 | all-reduce | flops 2 | bytes 16 | tf_op jit(solution)/shard_map/psum | solution.py:123
  794.4 11.7 %all-reduce.51 = (f32[]{:T(128)}, f32[]{:T(128)}) all-reduce(f32[]{:T(128)} %get-tuple-element.2990, f32[]{:T(128)} %get-tuple-element.2991), channel_id=1, replica_groups=mesh['gx'=4,'gy'=4,'gz'=2] {'gx'}, use_global_device_ids=true, to_apply=%region_45.0 | all-reduce | flops 2 | bytes 16 | tf_op jit(solution)/shard_map/psum | solution.py:122
  816.7 5.7 fusion.416
  859.2 13.0 %all-reduce.40 = (f32[]{:T(128)}, f32[]{:T(128)}) all-reduce(f32[]{:T(128)} %get-tuple-element.2969, f32[]{:T(128)} %get-tuple-element.2968), channel_id=1, replica_groups=mesh['gx'=4,'gy'=4,'gz'=2] {'gy','gz'}, use_global_device_ids=true, to_apply=%region_50.0 | all-reduce | flops 2 | bytes 16 | tf_op jit(solution)/shard_map/psum | solution.py:123
  872.3 11.6 %all-reduce.50 = (f32[]{:T(128)}, f32[]{:T(128)}) all-reduce(f32[]{:T(128)} %get-tuple-element.2988, f32[]{:T(128)} %get-tuple-element.2989), channel_id=1, replica_groups=mesh['gx'=4,'gy'=4,'gz'=2] {'gx'}, use_global_device_ids=true, to_apply=%region_51.0 | all-reduce | flops 2 | bytes 16 | tf_op jit(solution)/shard_map/psum | solution.py:122
  894.1 5.7 fusion.410
  936.7 13.1 %all-reduce.39 = (f32[]{:T(128)}, f32[]{:T(128)}) all-reduce(f32[]{:T(128)} %get-tuple-element.2967, f32[]{:T(128)} %get-tuple-element.2966), channel_id=1, replica_groups=mesh['gx'=4,'gy'=4,'gz'=2] {'gy','gz'}, use_global_device_ids=true, to_apply=%region_56.0 | all-reduce | flops 2 | bytes 16 | tf_op jit(solution)/shard_map/psum | solution.py:123
  949.8 11.7 %all-reduce.49 = (f32[]{:T(128)}, f32[]{:T(128)}) all-reduce(f32[]{:T(128)} %get-tuple-element.2986, f32[]{:T(128)} %get-tuple-element.2987), channel_id=1, replica_groups=mesh['gx'=4,'gy'=4,'gz'=2] {'gx'}, use_global_device_ids=true, to_apply=%region_57.0 | all-reduce | flops 2 | bytes 16 | tf_op jit(solution)/shard_map/psum | solution.py:122
  971.9 5.7 fusion.404
  1014.4 13.0 %all-reduce.38 = (f32[]{:T(128)}, f32[]{:T(128)}) all-reduce(f32[]{:T(128)} %get-tuple-element.2965, f32[]{:T(128)} %get-tuple-element.2964), channel_id=1, replica_groups=mesh['gx'=4,'gy'=4,'gz'=2] {'gy','gz'}, use_global_device_ids=true, to_apply=%region_62.0 | all-reduce | flops 2 | bytes 16 | tf_op jit(solution)/shard_map/psum | solution.py:123
  1027.5 11.6 %all-reduce.48 = (f32[]{:T(128)}, f32[]{:T(128)}) all-reduce(f32[]{:T(128)} %get-tuple-element.2984, f32[]{:T(128)} %get-tuple-element.2985), channel_id=1, replica_groups=mesh['gx'=4,'gy'=4,'gz'=2] {'gx'}, use_global_device_ids=true, to_apply=%region_63.0 | all-reduce | flops 2 | bytes 16 | tf_op jit(solution)/shard_map/psum | solution.py:122
  1049.3 5.7 fusion.398
  1091.9 13.1 %all-reduce.37 = (f32[]{:T(128)}, f32[]{:T(128)}) all-reduce(f32[]{:T(128)} %get-tuple-element.2963, f32[]{:T(128)} %get-tuple-element.2962), channel_id=1, replica_groups=mesh['gx'=4,'gy'=4,'gz'=2] {'gy','gz'}, use_global_device_ids=true, to_apply=%region_68.0 | all-reduce | flops 2 | bytes 16 | tf_op jit(solution)/shard_map/psum | solution.py:123
  1105.0 11.7 %all-reduce.47 = (f32[]{:T(128)}, f32[]{:T(128)}) all-reduce(f32[]{:T(128)} %get-tuple-element.2982, f32[]{:T(128)} %get-tuple-element.2983), channel_id=1, replica_groups=mesh['gx'=4,'gy'=4,'gz'=2] {'gx'}, use_global_device_ids=true, to_apply=%region_69.0 | all-reduce | flops 2 | bytes 16 | tf_op jit(solution)/shard_map/psum | solution.py:122
  (1716 shorter events, 760.2 us)
Async XLA Ops:
  0.6 51.9 %collective-permute-start = (f32[39,1,4,2,512]{4,3,2,1,0:T(2,128)}, f32[39,1,4,2,512]{4,3,2,1,0:T(2,128)S(1)}, u32[]{:S(2)}, u32[]{:S(2)}) collective-permute-start(f32[39,1,4,2,512]{4,3,2,1,0:T(2,128)} %bitcast.2152), channel_id=1, source_target_pairs={{0,8},{8,16},{16,24},{1,9},{9,17},{17,25},{2,10},{10,18},{18,26},{... | collective-permute-start | bytes 1916936 | tf_op jit(solution)/shard_map/ppermute | solution.py:34
  5.8 46.8 %collective-permute-start.1 = (f32[39,1,4,2,512]{4,3,2,1,0:T(2,128)}, f32[39,1,4,2,512]{4,3,2,1,0:T(2,128)S(1)}, u32[]{:S(2)}, u32[]{:S(2)}) collective-permute-start(f32[39,1,4,2,512]{4,3,2,1,0:T(2,128)} %bitcast.2153), channel_id=1, source_target_pairs={{8,0},{16,8},{24,16},{9,1},{17,9},{25,17},{10,2},{18,10},{26,18},{... | collective-permute-start | bytes 1916936 | tf_op jit(solution)/shard_map/ppermute | solution.py:35
  7.8 124.2 %collective-permute-start.6 = (f32[12,1,4,2,1]{0,2,4,3,1:T(4,128)S(1)}, f32[12,1,4,2,1]{0,2,4,3,1:T(4,128)}, u32[]{:S(2)}, u32[]{:S(2)}) collective-permute-start(f32[12,1,4,2,1]{0,2,4,3,1:T(4,128)S(1)} %bitcast.2434), channel_id=1, source_target_pairs={{0,8},{8,16},{16,24},{1,9},{9,17},{17,25},{2,10},{10,18},{18,26},{... | collective-permute-start | bytes 1160 | tf_op jit(solution)/shard_map/ppermute | solution.py:34
  12.9 119.0 %collective-permute-start.7 = (f32[12,1,4,2,1]{0,2,4,3,1:T(4,128)S(1)}, f32[12,1,4,2,1]{0,2,4,3,1:T(4,128)}, u32[]{:S(2)}, u32[]{:S(2)}) collective-permute-start(f32[12,1,4,2,1]{0,2,4,3,1:T(4,128)S(1)} %bitcast.2435), channel_id=1, source_target_pairs={{8,0},{16,8},{24,16},{9,1},{17,9},{25,17},{10,2},{18,10},{26,18},{... | collective-permute-start | bytes 1160 | tf_op jit(solution)/shard_map/ppermute | solution.py:35
  53.9 64.6 %collective-permute-start.2 = (f32[39,3,1,2,512]{4,3,2,1,0:T(2,128)}, f32[39,3,1,2,512]{4,3,2,1,0:T(2,128)S(1)}, u32[]{:S(2)}, u32[]{:S(2)}) collective-permute-start(f32[39,3,1,2,512]{4,3,2,1,0:T(2,128)} %get-tuple-element.3050), channel_id=1, source_target_pairs={{0,2},{2,4},{4,6},{1,3},{3,5},{5,7},{8,10},{10,12},{12,14},{9,11},... | collective-permute-start | bytes 1437704 | tf_op jit(solution)/shard_map/ppermute | solution.py:34
  57.4 61.1 %collective-permute-start.3 = (f32[39,3,1,2,512]{4,3,2,1,0:T(2,128)}, f32[39,3,1,2,512]{4,3,2,1,0:T(2,128)S(1)}, u32[]{:S(2)}, u32[]{:S(2)}) collective-permute-start(f32[39,3,1,2,512]{4,3,2,1,0:T(2,128)} %get-tuple-element.3051), channel_id=1, source_target_pairs={{2,0},{4,2},{6,4},{3,1},{5,3},{7,5},{10,8},{12,10},{14,12},{11,9},... | collective-permute-start | bytes 1437704 | tf_op jit(solution)/shard_map/ppermute | solution.py:35
  124.0 38.5 %collective-permute-start.4 = (f32[39,3,6,1,512]{4,3,2,1,0:T(1,128)}, f32[39,3,6,1,512]{4,3,2,1,0:T(1,128)}, u32[]{:S(2)}, u32[]{:S(2)}) collective-permute-start(f32[39,3,6,1,512]{4,3,2,1,0:T(1,128)} %get-tuple-element.3048), channel_id=1, source_target_pairs={{0,1},{2,3},{4,5},{6,7},{8,9},{10,11},{12,13},{14,15},{16,17},{18,... | collective-permute-start | bytes 4313096 | tf_op jit(solution)/shard_map/ppermute | solution.py:34
  126.4 36.1 %collective-permute-start.5 = (f32[39,3,6,1,512]{4,3,2,1,0:T(1,128)}, f32[39,3,6,1,512]{4,3,2,1,0:T(1,128)}, u32[]{:S(2)}, u32[]{:S(2)}) collective-permute-start(f32[39,3,6,1,512]{4,3,2,1,0:T(1,128)} %get-tuple-element.3049), channel_id=1, source_target_pairs={{1,0},{3,2},{5,4},{7,6},{9,8},{11,10},{13,12},{15,14},{17,16},{19,... | collective-permute-start | bytes 4313096 | tf_op jit(solution)/shard_map/ppermute | solution.py:35
  266.7 50.7 %collective-permute-start.12 = (f32[156,1,6,4]{0,3,2,1:T(4,128)S(1)}, f32[156,1,6,4]{0,3,2,1:T(4,128)S(1)}, u32[]{:S(2)}, u32[]{:S(2)}) collective-permute-start(f32[156,1,6,4]{0,3,2,1:T(4,128)S(1)} %get-tuple-element.3090), channel_id=1, source_target_pairs={{0,8},{8,16},{16,24},{1,9},{9,17},{17,25},{2,10},{10,18},{18,26},{... | collective-permute-start | bytes 44936 | tf_op jit(solution)/shard_map/ppermute | solution.py:34
  271.2 46.2 %collective-permute-start.13 = (f32[156,1,6,4]{0,3,2,1:T(4,128)S(1)}, f32[156,1,6,4]{0,3,2,1:T(4,128)S(1)}, u32[]{:S(2)}, u32[]{:S(2)}) collective-permute-start(f32[156,1,6,4]{0,3,2,1:T(4,128)S(1)} %get-tuple-element.3091), channel_id=1, source_target_pairs={{8,0},{16,8},{24,16},{9,1},{17,9},{25,17},{10,2},{18,10},{26,18},{... | collective-permute-start | bytes 44936 | tf_op jit(solution)/shard_map/ppermute | solution.py:35
  343.9 22.1 %collective-permute-start.18 = (f32[12,1,4,2]{0,3,2,1:T(2,128)S(1)}, f32[12,1,4,2]{0,3,2,1:T(2,128)S(1)}, u32[]{:S(2)}, u32[]{:S(2)}) collective-permute-start(f32[12,1,4,2]{0,3,2,1:T(2,128)S(1)} %bitcast.2227), channel_id=1, source_target_pairs={{8,0},{16,8},{24,16},{9,1},{17,9},{25,17},{10,2},{18,10},{26,18},{... | collective-permute-start | bytes 1160 | tf_op jit(solution)/shard_map/ppermute | solution.py:35
  345.2 20.9 %collective-permute-start.19 = (f32[12,1,4,2]{0,3,2,1:T(2,128)S(1)}, f32[12,1,4,2]{0,3,2,1:T(2,128)S(1)}, u32[]{:S(2)}, u32[]{:S(2)}) collective-permute-start(f32[12,1,4,2]{0,3,2,1:T(2,128)S(1)} %bitcast.2228), channel_id=1, source_target_pairs={{0,8},{8,16},{16,24},{1,9},{9,17},{17,25},{2,10},{10,18},{18,26},{... | collective-permute-start | bytes 1160 | tf_op jit(solution)/shard_map/ppermute | solution.py:34
  373.3 19.9 %collective-permute-start.22 = (f32[12,3,6,1]{0,3,2,1:T(1,128)S(1)}, f32[12,3,6,1]{0,3,2,1:T(1,128)S(1)}, u32[]{:S(2)}, u32[]{:S(2)}) collective-permute-start(f32[12,3,6,1]{0,3,2,1:T(1,128)S(1)} %get-tuple-element.3394), channel_id=1, source_target_pairs={{1,0},{3,2},{5,4},{7,6},{9,8},{11,10},{13,12},{15,14},{17,16},{19,... | collective-permute-start | bytes 2600 | tf_op jit(solution)/shard_map/ppermute | solution.py:35
  420.7 19.4 %collective-permute-start.30 = (f32[12,1,4,2]{0,3,2,1:T(2,128)S(1)}, f32[12,1,4,2]{0,3,2,1:T(2,128)S(1)}, u32[]{:S(2)}, u32[]{:S(2)}) collective-permute-start(f32[12,1,4,2]{0,3,2,1:T(2,128)S(1)} %bitcast.2238), channel_id=1, source_target_pairs={{8,0},{16,8},{24,16},{9,1},{17,9},{25,17},{10,2},{18,10},{26,18},{... | collective-permute-start | bytes 1160 | tf_op jit(solution)/shard_map/ppermute | solution.py:35
  447.3 21.0 %collective-permute-start.34 = (f32[12,3,6,1]{0,3,2,1:T(1,128)S(1)}, f32[12,3,6,1]{0,3,2,1:T(1,128)S(1)}, u32[]{:S(2)}, u32[]{:S(2)}) collective-permute-start(f32[12,3,6,1]{0,3,2,1:T(1,128)S(1)} %get-tuple-element.3391), channel_id=1, source_target_pairs={{1,0},{3,2},{5,4},{7,6},{9,8},{11,10},{13,12},{15,14},{17,16},{19,... | collective-permute-start | bytes 2600 | tf_op jit(solution)/shard_map/ppermute | solution.py:35
  448.6 19.7 %collective-permute-start.35 = (f32[12,3,6,1]{0,3,2,1:T(1,128)S(1)}, f32[12,3,6,1]{0,3,2,1:T(1,128)S(1)}, u32[]{:S(2)}, u32[]{:S(2)}) collective-permute-start(f32[12,3,6,1]{0,3,2,1:T(1,128)S(1)} %get-tuple-element.3390), channel_id=1, source_target_pairs={{0,1},{2,3},{4,5},{6,7},{8,9},{10,11},{12,13},{14,15},{16,17},{18,... | collective-permute-start | bytes 2600 | tf_op jit(solution)/shard_map/ppermute | solution.py:34
  499.8 19.3 %collective-permute-start.42 = (f32[12,1,4,2]{0,3,2,1:T(2,128)S(1)}, f32[12,1,4,2]{0,3,2,1:T(2,128)S(1)}, u32[]{:S(2)}, u32[]{:S(2)}) collective-permute-start(f32[12,1,4,2]{0,3,2,1:T(2,128)S(1)} %bitcast.2249), channel_id=1, source_target_pairs={{8,0},{16,8},{24,16},{9,1},{17,9},{25,17},{10,2},{18,10},{26,18},{... | collective-permute-start | bytes 1160 | tf_op jit(solution)/shard_map/ppermute | solution.py:35
  526.3 20.4 %collective-permute-start.46 = (f32[12,3,6,1]{0,3,2,1:T(1,128)S(1)}, f32[12,3,6,1]{0,3,2,1:T(1,128)S(1)}, u32[]{:S(2)}, u32[]{:S(2)}) collective-permute-start(f32[12,3,6,1]{0,3,2,1:T(1,128)S(1)} %get-tuple-element.3388), channel_id=1, source_target_pairs={{1,0},{3,2},{5,4},{7,6},{9,8},{11,10},{13,12},{15,14},{17,16},{19,... | collective-permute-start | bytes 2600 | tf_op jit(solution)/shard_map/ppermute | solution.py:35
  577.4 19.3 %collective-permute-start.54 = (f32[12,1,4,2]{0,3,2,1:T(2,128)S(1)}, f32[12,1,4,2]{0,3,2,1:T(2,128)S(1)}, u32[]{:S(2)}, u32[]{:S(2)}) collective-permute-start(f32[12,1,4,2]{0,3,2,1:T(2,128)S(1)} %bitcast.2260), channel_id=1, source_target_pairs={{8,0},{16,8},{24,16},{9,1},{17,9},{25,17},{10,2},{18,10},{26,18},{... | collective-permute-start | bytes 1160 | tf_op jit(solution)/shard_map/ppermute | solution.py:35
  603.9 20.4 %collective-permute-start.58 = (f32[12,3,6,1]{0,3,2,1:T(1,128)S(1)}, f32[12,3,6,1]{0,3,2,1:T(1,128)S(1)}, u32[]{:S(2)}, u32[]{:S(2)}) collective-permute-start(f32[12,3,6,1]{0,3,2,1:T(1,128)S(1)} %get-tuple-element.3385), channel_id=1, source_target_pairs={{1,0},{3,2},{5,4},{7,6},{9,8},{11,10},{13,12},{15,14},{17,16},{19,... | collective-permute-start | bytes 2600 | tf_op jit(solution)/shard_map/ppermute | solution.py:35
  655.0 19.5 %collective-permute-start.66 = (f32[12,1,4,2]{0,3,2,1:T(2,128)S(1)}, f32[12,1,4,2]{0,3,2,1:T(2,128)S(1)}, u32[]{:S(2)}, u32[]{:S(2)}) collective-permute-start(f32[12,1,4,2]{0,3,2,1:T(2,128)S(1)} %bitcast.2271), channel_id=1, source_target_pairs={{8,0},{16,8},{24,16},{9,1},{17,9},{25,17},{10,2},{18,10},{26,18},{... | collective-permute-start | bytes 1160 | tf_op jit(solution)/shard_map/ppermute | solution.py:35
  681.7 20.4 %collective-permute-start.70 = (f32[12,3,6,1]{0,3,2,1:T(1,128)S(1)}, f32[12,3,6,1]{0,3,2,1:T(1,128)S(1)}, u32[]{:S(2)}, u32[]{:S(2)}) collective-permute-start(f32[12,3,6,1]{0,3,2,1:T(1,128)S(1)} %get-tuple-element.3382), channel_id=1, source_target_pairs={{1,0},{3,2},{5,4},{7,6},{9,8},{11,10},{13,12},{15,14},{17,16},{19,... | collective-permute-start | bytes 2600 | tf_op jit(solution)/shard_map/ppermute | solution.py:35
  732.6 19.3 %collective-permute-start.78 = (f32[12,1,4,2]{0,3,2,1:T(2,128)S(1)}, f32[12,1,4,2]{0,3,2,1:T(2,128)S(1)}, u32[]{:S(2)}, u32[]{:S(2)}) collective-permute-start(f32[12,1,4,2]{0,3,2,1:T(2,128)S(1)} %bitcast.2282), channel_id=1, source_target_pairs={{8,0},{16,8},{24,16},{9,1},{17,9},{25,17},{10,2},{18,10},{26,18},{... | collective-permute-start | bytes 1160 | tf_op jit(solution)/shard_map/ppermute | solution.py:35
  759.1 20.4 %collective-permute-start.82 = (f32[12,3,6,1]{0,3,2,1:T(1,128)S(1)}, f32[12,3,6,1]{0,3,2,1:T(1,128)S(1)}, u32[]{:S(2)}, u32[]{:S(2)}) collective-permute-start(f32[12,3,6,1]{0,3,2,1:T(1,128)S(1)} %get-tuple-element.3379), channel_id=1, source_target_pairs={{1,0},{3,2},{5,4},{7,6},{9,8},{11,10},{13,12},{15,14},{17,16},{19,... | collective-permute-start | bytes 2600 | tf_op jit(solution)/shard_map/ppermute | solution.py:35
  810.2 19.7 %collective-permute-start.90 = (f32[12,1,4,2]{0,3,2,1:T(2,128)S(1)}, f32[12,1,4,2]{0,3,2,1:T(2,128)S(1)}, u32[]{:S(2)}, u32[]{:S(2)}) collective-permute-start(f32[12,1,4,2]{0,3,2,1:T(2,128)S(1)} %bitcast.2293), channel_id=1, source_target_pairs={{8,0},{16,8},{24,16},{9,1},{17,9},{25,17},{10,2},{18,10},{26,18},{... | collective-permute-start | bytes 1160 | tf_op jit(solution)/shard_map/ppermute | solution.py:35
  837.1 20.4 %collective-permute-start.94 = (f32[12,3,6,1]{0,3,2,1:T(1,128)S(1)}, f32[12,3,6,1]{0,3,2,1:T(1,128)S(1)}, u32[]{:S(2)}, u32[]{:S(2)}) collective-permute-start(f32[12,3,6,1]{0,3,2,1:T(1,128)S(1)} %get-tuple-element.3376), channel_id=1, source_target_pairs={{1,0},{3,2},{5,4},{7,6},{9,8},{11,10},{13,12},{15,14},{17,16},{19,... | collective-permute-start | bytes 2600 | tf_op jit(solution)/shard_map/ppermute | solution.py:35
  888.0 19.3 %collective-permute-start.102 = (f32[12,1,4,2]{0,3,2,1:T(2,128)S(1)}, f32[12,1,4,2]{0,3,2,1:T(2,128)S(1)}, u32[]{:S(2)}, u32[]{:S(2)}) collective-permute-start(f32[12,1,4,2]{0,3,2,1:T(2,128)S(1)} %bitcast.2304), channel_id=1, source_target_pairs={{8,0},{16,8},{24,16},{9,1},{17,9},{25,17},{10,2},{18,10},{26,18},{... | collective-permute-start | bytes 1160 | tf_op jit(solution)/shard_map/ppermute | solution.py:35
  914.5 20.4 %collective-permute-start.106 = (f32[12,3,6,1]{0,3,2,1:T(1,128)S(1)}, f32[12,3,6,1]{0,3,2,1:T(1,128)S(1)}, u32[]{:S(2)}, u32[]{:S(2)}) collective-permute-start(f32[12,3,6,1]{0,3,2,1:T(1,128)S(1)} %get-tuple-element.3373), channel_id=1, source_target_pairs={{1,0},{3,2},{5,4},{7,6},{9,8},{11,10},{13,12},{15,14},{17,16},{19,... | collective-permute-start | bytes 2600 | tf_op jit(solution)/shard_map/ppermute | solution.py:35
  965.6 19.4 %collective-permute-start.114 = (f32[12,1,4,2]{0,3,2,1:T(2,128)S(1)}, f32[12,1,4,2]{0,3,2,1:T(2,128)S(1)}, u32[]{:S(2)}, u32[]{:S(2)}) collective-permute-start(f32[12,1,4,2]{0,3,2,1:T(2,128)S(1)} %bitcast.2315), channel_id=1, source_target_pairs={{8,0},{16,8},{24,16},{9,1},{17,9},{25,17},{10,2},{18,10},{26,18},{... | collective-permute-start | bytes 1160 | tf_op jit(solution)/shard_map/ppermute | solution.py:35
  992.3 20.4 %collective-permute-start.118 = (f32[12,3,6,1]{0,3,2,1:T(1,128)S(1)}, f32[12,3,6,1]{0,3,2,1:T(1,128)S(1)}, u32[]{:S(2)}, u32[]{:S(2)}) collective-permute-start(f32[12,3,6,1]{0,3,2,1:T(1,128)S(1)} %get-tuple-element.3370), channel_id=1, source_target_pairs={{1,0},{3,2},{5,4},{7,6},{9,8},{11,10},{13,12},{15,14},{17,16},{19,... | collective-permute-start | bytes 2600 | tf_op jit(solution)/shard_map/ppermute | solution.py:35
  1043.2 19.3 %collective-permute-start.126 = (f32[12,1,4,2]{0,3,2,1:T(2,128)S(1)}, f32[12,1,4,2]{0,3,2,1:T(2,128)S(1)}, u32[]{:S(2)}, u32[]{:S(2)}) collective-permute-start(f32[12,1,4,2]{0,3,2,1:T(2,128)S(1)} %bitcast.2326), channel_id=1, source_target_pairs={{8,0},{16,8},{24,16},{9,1},{17,9},{25,17},{10,2},{18,10},{26,18},{... | collective-permute-start | bytes 1160 | tf_op jit(solution)/shard_map/ppermute | solution.py:35
  1069.7 20.4 %collective-permute-start.130 = (f32[12,3,6,1]{0,3,2,1:T(1,128)S(1)}, f32[12,3,6,1]{0,3,2,1:T(1,128)S(1)}, u32[]{:S(2)}, u32[]{:S(2)}) collective-permute-start(f32[12,3,6,1]{0,3,2,1:T(1,128)S(1)} %get-tuple-element.3367), channel_id=1, source_target_pairs={{1,0},{3,2},{5,4},{7,6},{9,8},{11,10},{13,12},{15,14},{17,16},{19,... | collective-permute-start | bytes 2600 | tf_op jit(solution)/shard_map/ppermute | solution.py:35
  (293 other events, 2916.5 us)
